TPU v7x, 512 devices: a whole 4x8x8 slice. The times are simulated.
512 devices in a mesh: pipe: 4 (over x), expert: 128 (over y, z, core).
Axes of the slice: x: 4, y: 8, z: 8, core: 2. Of those that a mesh axis runs over, the one named last changes fastest.
Arguments:
- out_grad: bfloat16 [4, 2, 8192, 7168], P('pipe', None, 'expert'), may hold values from -1.5 to 1.5
- expert_ids: int32 [4, 2, 8192, 8], P('pipe', None, 'expert'), may hold values from 0 to 383, as said below
- gate_values: float32 [4, 2, 8192, 8], P('pipe', None, 'expert'), may hold values from 0.05 to 1
- down_tiles: bfloat16 [4, 128, 512, 896], P('pipe', 'expert'), may hold values from -0.125 to 0.125
- hidden_saved: bfloat16 [4, 2, 512, 8192], P('pipe', None, None, 'expert'), may hold values from -0.59765625 to 0.59765625
Outputs:
- hidden_grad: bfloat16 [4, 2, 512, 8192], P('pipe', None, None, 'expert')
- down_grad: bfloat16 [4, 128, 512, 896], P('pipe', 'expert')
- gate_grad: float32 [4, 2, 8192, 8], P('pipe', None, 'expert')
Inputs may be any that keep to these rules, and one draw needn't show every extreme that they name: `expert_ids`: each row names 8 different experts. The experts of the window are those below 4. Among the 64 rows of one device in one micro-batch of one section, no window expert is named by more than 4 rows, and in every micro-batch of every section one window expert is named by exactly 4 rows of every device.
All inputs are finite; a program needn't handle non-finite values.
Results may differ from a plain program's by a relative error of at most 0.0057.
Values may be sent and summed in bfloat16 or wider, within the bound.
A program may use at most 64 MiB of HBM per device.

v0:
```python
import jax
import jax.numpy as jnp
from jax import lax
from jax.sharding import PartitionSpec as P

MICRO = 2
TOK_DEV = 64
CAP = 4


def passed_along(shard, axis, by):
    peers = lax.axis_size(axis)
    return lax.ppermute(shard, axis, [(i, (i + by) % peers) for i in range(peers)])


def swapped(block, axis, distance):
    count = lax.axis_size(axis)
    route = []
    for low in range(count):
        high = low | 1 << distance
        if high != low and high < count:
            route += [(low, high), (high, low)]
    return lax.ppermute(block, axis, route)


def body(out_grad, expert_ids, gate_values, down_tiles, hidden_saved):
    devices = lax.axis_size("expert")
    hidden_split = 4
    feature_split = min(8, devices // 4)
    group_size = hidden_split * feature_split
    windows = devices // group_size
    low_bits = feature_split.bit_length() - 1
    position = lax.axis_index("expert")
    weight = down_tiles[0, 0]
    tile_rows = weight.shape[0]
    tile_cols = weight.shape[1]
    slot_count = devices * CAP
    grad_total = jnp.zeros((tile_rows, tile_cols), jnp.float32)
    hidden_list = []
    score_list = []
    table_list = []
    for micro_step in range(MICRO):
        token_rows = passed_along(out_grad[0, micro_step], "pipe", -1)
        routing = expert_ids[0, micro_step]
        gate_rows = gate_values[0, micro_step]
        named_mask = routing[:, :, None] == jnp.arange(windows, dtype=jnp.int32)[None, None, :]
        hit_count = jnp.any(named_mask, axis=1).astype(jnp.int32)
        slot_rank = jnp.cumsum(hit_count, axis=0) - hit_count
        pick_table = (
            slot_rank.T[:, None, :] == jnp.arange(CAP, dtype=jnp.int32)[None, :, None]
        ) & (hit_count.T[:, None, :] == 1)
        gate_pick = jnp.sum(jnp.where(named_mask, gate_rows[:, :, None], jnp.float32(0.0)), axis=1)
        buffer = jnp.dot(
            pick_table.astype(jnp.bfloat16).reshape(windows * CAP, TOK_DEV),
            token_rows,
            preferred_element_type=jnp.float32,
        ).astype(jnp.bfloat16)
        gate_buffer = jnp.sum(
            jnp.where(pick_table, gate_pick.T[:, None, :], jnp.float32(0.0)), axis=2
        )
        gate_out = (
            jnp.broadcast_to(gate_buffer[:, None, :], (windows, group_size, CAP))
            .reshape(slot_count)
            .astype(jnp.bfloat16)
        )
        arranged = buffer.reshape(windows, CAP, feature_split, tile_cols).transpose(0, 2, 1, 3)
        outgoing = jnp.broadcast_to(
            arranged[:, None], (windows, hidden_split, feature_split, CAP, tile_cols)
        ).reshape(slot_count, tile_cols)
        received, gate_arrived = (
            lax.all_to_all(outgoing, "expert", split_axis=0, concat_axis=0, tiled=True),
            lax.all_to_all(gate_out, "expert", split_axis=0, concat_axis=0, tiled=True),
        )
        gate_wide = gate_arrived.astype(jnp.float32)
        hidden_full = hidden_saved[0, micro_step]
        for level_bit in range(low_bits):
            partner_hidden = swapped(hidden_full, "expert", level_bit)
            upper_side = position // 2**level_bit % 2 == 1
            hidden_full = jnp.where(
                upper_side,
                jnp.concatenate([partner_hidden, hidden_full], axis=1),
                jnp.concatenate([hidden_full, partner_hidden], axis=1),
            )
        partial_value = lax.dot_general(
            received, weight, (((1,), (1,)), ((), ())), preferred_element_type=jnp.float32
        )
        score_part = jnp.sum(hidden_full.astype(jnp.float32) * partial_value, axis=1)
        summed = partial_value
        for level in range(low_bits):
            level_bit = low_bits - 1 - level
            width = summed.shape[1] // 2
            side = position // 2**level_bit % 2
            kept_cols = lax.dynamic_slice_in_dim(summed, side * width, width, 1)
            given_cols = lax.dynamic_slice_in_dim(summed, (1 - side) * width, width, 1)
            summed = kept_cols + swapped(given_cols, "expert", level_bit)
        hidden_list.append((gate_wide[:, None] * summed).astype(jnp.bfloat16))
        scaled = (gate_wide[:, None] * hidden_full.astype(jnp.float32)).astype(jnp.bfloat16)
        grad_total = grad_total + lax.dot_general(
            scaled, received, (((0,), (0,)), ((), ())), preferred_element_type=jnp.float32
        )
        score_list.append(score_part.reshape(devices, CAP))
        table_list.append((named_mask, pick_table))
    returned = [
        lax.all_to_all(score_block, "expert", split_axis=0, concat_axis=0, tiled=True)
        for score_block in score_list
    ]
    gate_list = []
    for micro_step in range(MICRO):
        named_mask, pick_table = table_list[micro_step]
        totals = returned[micro_step].reshape(windows, group_size, CAP).sum(axis=1)
        token_score = jnp.sum(jnp.where(pick_table, totals[:, :, None], jnp.float32(0.0)), axis=1)
        gate_list.append(
            jnp.sum(jnp.where(named_mask, token_score.T[:, None, :], jnp.float32(0.0)), axis=2)
        )
    hidden_grad = jnp.stack(hidden_list)[None]
    down_grad = grad_total.astype(jnp.bfloat16)[None, None]
    gate_grad = jnp.stack(gate_list)[None]
    return (hidden_grad, down_grad, gate_grad)


def solution(mesh):
    return jax.shard_map(
        body,
        mesh=mesh,
        in_specs=(
            P("pipe", None, "expert", None),
            P("pipe", None, "expert", None),
            P("pipe", None, "expert", None),
            P("pipe", "expert", None, None),
            P("pipe", None, None, "expert"),
        ),
        out_specs=(
            P("pipe", None, None, "expert"),
            P("pipe", "expert", None, None),
            P("pipe", None, "expert", None),
        ),
        check_vma=False,
    )
```

profile of v0, /device:TPU:7, one launch (start us, length us, event | category | flops | bytes accessed | tf_op | source)
XLA Modules:
  0.0 266.7 jit_solution(1815225977127254673)
XLA Ops:
  2.3 2.5 collective-permute-start.4
  5.3 18.8 %collective-permute-done.4 = bf16[64,7168]{1,0:T(8,128)(2,1)} collective-permute-done((bf16[64,7168]{1,0:T(8,128)(2,1)S(1)}, bf16[64,7168]{1,0:T(8,128)(2,1)}, u32[]{:S(2)}, u32[]{:S(2)}) %collective-permute-start.4) | collective-permute-done | bytes 917536 | tf_op jit(solution)/shard_map/ppermute | solution.py:13
  26.9 21.1 %all-to-all-start.3 = ((bf16[128,4,896]{2,1,0:T(4,128)(2,1)}), bf16[128,4,896]{2,1,0:T(4,128)(2,1)S(1)}, u32[]{:S(2)}, u32[]{:S(2)}) async-start(bf16[128,4,896]{2,1,0:T(4,128)(2,1)} %bitcast.21), calls=%async_computation.3 | async-start | bytes 1835008 | tf_op jit(solution)/shard_map/all_to_all | solution.py:71
  50.4 21.8 %collective-permute-done = bf16[64,7168]{1,0:T(8,128)(2,1)} collective-permute-done((bf16[64,7168]{1,0:T(8,128)(2,1)S(1)}, bf16[64,7168]{1,0:T(8,128)(2,1)}, u32[]{:S(2)}, u32[]{:S(2)}) %collective-permute-start) | collective-permute-done | bytes 917536 | tf_op jit(solution)/shard_map/ppermute | solution.py:13
  77.1 13.3 %all-to-all-start.1 = ((bf16[128,4,896]{2,1,0:T(4,128)(2,1)}), bf16[128,4,896]{2,1,0:T(4,128)(2,1)S(1)}, u32[]{:S(2)}, u32[]{:S(2)}) async-start(bf16[128,4,896]{2,1,0:T(4,128)(2,1)} %bitcast.83), calls=%async_computation.1 | async-start | bytes 1835008 | tf_op jit(solution)/shard_map/all_to_all | solution.py:71
  90.4 2.8 %collective-permute-start.11 = (bf16[512,64]{0,1:T(8,128)(2,1)S(1)}, bf16[512,64]{0,1:T(8,128)(2,1)S(1)}, u32[]{:S(2)}, u32[]{:S(2)}) collective-permute-start(bf16[512,64]{0,1:T(8,128)(2,1)S(1)} %get-tuple-element.10), channel_id=1, source_target_pairs={{0,1},{1,0},{2,3},{3,2},{4,5},{5,4},{6,7},{7,6},{8,9},{9,8},{10,11... | collective-permute-start | bytes 196616 | tf_op jit(solution)/shard_map/ppermute | solution.py:23
  95.2 2.9 %collective-permute-start.12 = (bf16[512,128]{0,1:T(8,128)(2,1)S(1)}, bf16[512,128]{0,1:T(8,128)(2,1)S(1)}, u32[]{:S(2)}, u32[]{:S(2)}) collective-permute-start(bf16[512,128]{0,1:T(8,128)(2,1)S(1)} %maximum_select_fusion.5), channel_id=1, source_target_pairs={{0,2},{2,0},{1,3},{3,1},{4,6},{6,4},{5,7},{7,5},{8,10},{10,8},{9,1... | collective-permute-start | bytes 393224 | tf_op jit(solution)/shard_map/ppermute | solution.py:23
  100.6 13.7 %collective-permute-done.12 = bf16[512,128]{0,1:T(8,128)(2,1)S(1)} collective-permute-done((bf16[512,128]{0,1:T(8,128)(2,1)S(1)}, bf16[512,128]{0,1:T(8,128)(2,1)S(1)}, u32[]{:S(2)}, u32[]{:S(2)}) %collective-permute-start.12) | collective-permute-done | bytes 131104 | tf_op jit(solution)/shard_map/ppermute | solution.py:23
  114.4 5.7 %collective-permute-start.13 = (bf16[512,256]{0,1:T(8,128)(2,1)S(1)}, bf16[512,256]{0,1:T(8,128)(2,1)}, u32[]{:S(2)}, u32[]{:S(2)}) collective-permute-start(bf16[512,256]{0,1:T(8,128)(2,1)S(1)} %maximum_select_fusion.3), channel_id=1, source_target_pairs={{0,4},{4,0},{1,5},{5,1},{2,6},{6,2},{3,7},{7,3},{8,12},{12,8},{9,1... | collective-permute-start | bytes 786440 | tf_op jit(solution)/shard_map/ppermute | solution.py:23
  124.4 13.5 %collective-permute-done.13 = bf16[512,256]{0,1:T(8,128)(2,1)} collective-permute-done((bf16[512,256]{0,1:T(8,128)(2,1)S(1)}, bf16[512,256]{0,1:T(8,128)(2,1)}, u32[]{:S(2)}, u32[]{:S(2)}) %collective-permute-start.13) | collective-permute-done | bytes 262176 | tf_op jit(solution)/shard_map/ppermute | solution.py:23
  144.5 13.3 %all-to-all-start.5 = ((f32[128,1,4]{2,1,0:T(1,128)}), f32[128,1,4]{2,1,0:T(1,128)S(1)}, u32[]{:S(2)}, u32[]{:S(2)}) async-start(f32[128,1,4]{2,1,0:T(1,128)} %bitcast.31), calls=%async_computation.5 | async-start | bytes 131072 | tf_op jit(solution)/shard_map/all_to_all | solution.py:104
  162.6 4.2 %collective-permute-start.1 = (f32[512,256]{0,1:T(8,128)}, f32[512,256]{0,1:T(8,128)}, u32[]{:S(2)}, u32[]{:S(2)}) collective-permute-start(f32[512,256]{0,1:T(8,128)} %constant_dynamic-slice_fusion.5), channel_id=1, source_target_pairs={{0,4},{4,0},{1,5},{5,1},{2,6},{6,2},{3,7},{7,3},{8,12},{12,8},{9,1... | collective-permute-start | bytes 1572872 | tf_op jit(solution)/shard_map/ppermute | solution.py:23
  166.8 17.2 %all-to-all-done.5 = f32[128,1,4]{2,1,0:T(1,128)S(1)} async-done(((f32[128,1,4]{2,1,0:T(1,128)}), f32[128,1,4]{2,1,0:T(1,128)S(1)}, u32[]{:S(2)}, u32[]{:S(2)}) %all-to-all-start.5) | async-done | bytes 2080 | tf_op jit(solution)/shard_map/all_to_all | solution.py:104
  184.0 8.3 %all-to-all-start.4 = ((f32[128,1,4]{2,1,0:T(1,128)}), f32[128,1,4]{2,1,0:T(1,128)S(1)}, u32[]{:S(2)}, u32[]{:S(2)}) async-start(f32[128,1,4]{2,1,0:T(1,128)} %bitcast.27), calls=%async_computation.4 | async-start | bytes 131072 | tf_op jit(solution)/shard_map/all_to_all | solution.py:104
  193.0 10.8 %all-to-all-done.4 = f32[128,1,4]{2,1,0:T(1,128)S(1)} async-done(((f32[128,1,4]{2,1,0:T(1,128)}), f32[128,1,4]{2,1,0:T(1,128)S(1)}, u32[]{:S(2)}, u32[]{:S(2)}) %all-to-all-start.4) | async-done | bytes 2080 | tf_op jit(solution)/shard_map/all_to_all | solution.py:104
  207.0 5.7 %all-to-all-start.2 = ((bf16[128,4,1]{1,2,0:T(2,128)(2,1)}), bf16[128,4,1]{1,2,0:T(2,128)(2,1)S(1)}, u32[]{:S(2)}, u32[]{:S(2)}) async-start(bf16[128,4,1]{1,2,0:T(2,128)(2,1)} %copy.64), calls=%async_computation.2 | async-start | bytes 131072 | tf_op jit(solution)/shard_map/all_to_all | solution.py:72
  215.1 9.2 %all-to-all-done.2 = bf16[128,4,1]{1,2,0:T(2,128)(2,1)S(1)} async-done(((bf16[128,4,1]{1,2,0:T(2,128)(2,1)}), bf16[128,4,1]{1,2,0:T(2,128)(2,1)S(1)}, u32[]{:S(2)}, u32[]{:S(2)}) %all-to-all-start.2) | async-done | bytes 1056 | tf_op jit(solution)/shard_map/all_to_all | solution.py:72
  224.4 5.6 %all-to-all-start = ((bf16[128,4,1]{1,2,0:T(2,128)(2,1)}), bf16[128,4,1]{1,2,0:T(2,128)(2,1)S(1)}, u32[]{:S(2)}, u32[]{:S(2)}) async-start(bf16[128,4,1]{1,2,0:T(2,128)(2,1)} %copy.58), calls=%async_computation | async-start | bytes 131072 | tf_op jit(solution)/shard_map/all_to_all | solution.py:72
  231.7 9.9 %all-to-all-done = bf16[128,4,1]{1,2,0:T(2,128)(2,1)S(1)} async-done(((bf16[128,4,1]{1,2,0:T(2,128)(2,1)}), bf16[128,4,1]{1,2,0:T(2,128)(2,1)S(1)}, u32[]{:S(2)}, u32[]{:S(2)}) %all-to-all-start) | async-done | bytes 1056 | tf_op jit(solution)/shard_map/all_to_all | solution.py:72
  244.0 2.8 %fusion = bf16[1,1,512,896]{3,2,1,0:T(8,128)(2,1)} fusion(f32[512,896]{1,0:T(8,128)S(1)} %fusion.10, bf16[512,896]{1,0:T(8,128)(2,1)S(1)} %copy-done.3, f32[512]{0:T(512)S(1)} %reshape.111, bf16[512,256]{0,1:T(8,128)(2,1)S(1)} %copy-done.6, bf16[512,256]{0,1:T(8,128)(2,1)} %collective-permute-done.13, pred[]{:T(512)S(6)} %eq.142), kind=kOutput, calls=%fused_computation.3 | convolution fusion | flops 473825280 | bytes 4196353 | tf_op jit(solution)/shard_map/dot_general | solution.py:98
  250.5 2.8 %collective-permute-start.2 = (f32[512,128]{0,1:T(8,128)S(1)}, f32[512,128]{0,1:T(8,128)S(1)}, u32[]{:S(2)}, u32[]{:S(2)}) collective-permute-start(f32[512,128]{0,1:T(8,128)S(1)} %constant_dynamic-slice_fusion.4), channel_id=1, source_target_pairs={{0,2},{2,0},{1,3},{3,1},{4,6},{6,4},{5,7},{7,5},{8,10},{10,8},{9,1... | collective-permute-start | bytes 786440 | tf_op jit(solution)/shard_map/ppermute | solution.py:23
  253.3 2.7 %collective-permute-done.6 = f32[512,128]{0,1:T(8,128)S(1)} collective-permute-done((f32[512,128]{0,1:T(8,128)S(1)}, f32[512,128]{0,1:T(8,128)S(1)}, u32[]{:S(2)}, u32[]{:S(2)}) %collective-permute-start.6) | collective-permute-done | bytes 262176 | tf_op jit(solution)/shard_map/ppermute | solution.py:23
  256.1 4.3 %collective-permute-start.7 = (f32[512,64]{0,1:T(8,128)S(1)}, f32[512,64]{0,1:T(8,128)S(1)}, u32[]{:S(2)}, u32[]{:S(2)}) collective-permute-start(f32[512,64]{0,1:T(8,128)S(1)} %constant_dynamic-slice_fusion), channel_id=1, source_target_pairs={{0,1},{1,0},{2,3},{3,2},{4,5},{5,4},{6,7},{7,6},{8,9},{9,8},{10,11... | collective-permute-start | bytes 393224 | tf_op jit(solution)/shard_map/ppermute | solution.py:23
  261.8 3.3 %collective-permute-start.3 = (f32[512,64]{0,1:T(8,128)S(1)}, f32[512,64]{0,1:T(8,128)S(1)}, u32[]{:S(2)}, u32[]{:S(2)}) collective-permute-start(f32[512,64]{0,1:T(8,128)S(1)} %constant_dynamic-slice_fusion.3), channel_id=1, source_target_pairs={{0,1},{1,0},{2,3},{3,2},{4,5},{5,4},{6,7},{7,6},{8,9},{9,8},{10,11... | collective-permute-start | bytes 393224 | tf_op jit(solution)/shard_map/ppermute | solution.py:23
  (119 shorter events, 49.2 us)
Async XLA Ops:
  0.6 137.3 %copy-start = (bf16[1,1,512,896]{3,2,1,0:T(8,128)(2,1)S(1)}, bf16[1,1,512,896]{3,2,1,0:T(8,128)(2,1)}, u32[]{:S(2)}) copy-start(bf16[1,1,512,896]{3,2,1,0:T(8,128)(2,1)} %param.8) | copy-start | bytes 2752516
  2.3 21.8 %collective-permute-start.4 = (bf16[64,7168]{1,0:T(8,128)(2,1)S(1)}, bf16[64,7168]{1,0:T(8,128)(2,1)}, u32[]{:S(2)}, u32[]{:S(2)}) collective-permute-start(bf16[64,7168]{1,0:T(8,128)(2,1)S(1)} %get-tuple-element.8), channel_id=1, source_target_pairs={{0,384},{128,0},{256,128},{384,256},{1,385},{129,1},{257,129},{385... | collective-permute-start | bytes 2752520 | tf_op jit(solution)/shard_map/ppermute | solution.py:13
  26.9 49.0 %all-to-all-start.3 = ((bf16[128,4,896]{2,1,0:T(4,128)(2,1)}), bf16[128,4,896]{2,1,0:T(4,128)(2,1)S(1)}, u32[]{:S(2)}, u32[]{:S(2)}) async-start(bf16[128,4,896]{2,1,0:T(4,128)(2,1)} %bitcast.21), calls=%async_computation.3 | async-start | bytes 1835008 | tf_op jit(solution)/shard_map/all_to_all | solution.py:71
  48.0 24.2 %collective-permute-start = (bf16[64,7168]{1,0:T(8,128)(2,1)S(1)}, bf16[64,7168]{1,0:T(8,128)(2,1)}, u32[]{:S(2)}, u32[]{:S(2)}) collective-permute-start(bf16[64,7168]{1,0:T(8,128)(2,1)S(1)} %get-tuple-element.7), channel_id=1, source_target_pairs={{0,384},{128,0},{256,128},{384,256},{1,385},{129,1},{257,129},{385... | collective-permute-start | bytes 2752520 | tf_op jit(solution)/shard_map/ppermute | solution.py:13
  77.1 43.0 %copy-start.10 = (f32[1,2,64,8]{2,3,1,0:T(8,128)S(1)}, f32[1,2,64,8]{2,3,1,0:T(8,128)}, u32[]{:S(2)}) copy-start(f32[1,2,64,8]{2,3,1,0:T(8,128)} %param.7) | copy-start | bytes 12292
  77.1 67.4 %all-to-all-start.1 = ((bf16[128,4,896]{2,1,0:T(4,128)(2,1)}), bf16[128,4,896]{2,1,0:T(4,128)(2,1)S(1)}, u32[]{:S(2)}, u32[]{:S(2)}) async-start(bf16[128,4,896]{2,1,0:T(4,128)(2,1)} %bitcast.83), calls=%async_computation.1 | async-start | bytes 1835008 | tf_op jit(solution)/shard_map/all_to_all | solution.py:71
  90.4 4.8 %collective-permute-start.11 = (bf16[512,64]{0,1:T(8,128)(2,1)S(1)}, bf16[512,64]{0,1:T(8,128)(2,1)S(1)}, u32[]{:S(2)}, u32[]{:S(2)}) collective-permute-start(bf16[512,64]{0,1:T(8,128)(2,1)S(1)} %get-tuple-element.10), channel_id=1, source_target_pairs={{0,1},{1,0},{2,3},{3,2},{4,5},{5,4},{6,7},{7,6},{8,9},{9,8},{10,11... | collective-permute-start | bytes 196616 | tf_op jit(solution)/shard_map/ppermute | solution.py:23
  93.2 5.0 %collective-permute-start.8 = (bf16[512,64]{0,1:T(8,128)(2,1)S(1)}, bf16[512,64]{0,1:T(8,128)(2,1)S(1)}, u32[]{:S(2)}, u32[]{:S(2)}) collective-permute-start(bf16[512,64]{0,1:T(8,128)(2,1)S(1)} %get-tuple-element.9), channel_id=1, source_target_pairs={{0,1},{1,0},{2,3},{3,2},{4,5},{5,4},{6,7},{7,6},{8,9},{9,8},{10,11... | collective-permute-start | bytes 196616 | tf_op jit(solution)/shard_map/ppermute | solution.py:23
  95.2 19.1 %collective-permute-start.12 = (bf16[512,128]{0,1:T(8,128)(2,1)S(1)}, bf16[512,128]{0,1:T(8,128)(2,1)S(1)}, u32[]{:S(2)}, u32[]{:S(2)}) collective-permute-start(bf16[512,128]{0,1:T(8,128)(2,1)S(1)} %maximum_select_fusion.5), channel_id=1, source_target_pairs={{0,2},{2,0},{1,3},{3,1},{4,6},{6,4},{5,7},{7,5},{8,10},{10,8},{9,1... | collective-permute-start | bytes 393224 | tf_op jit(solution)/shard_map/ppermute | solution.py:23
  98.2 22.5 %collective-permute-start.9 = (bf16[512,128]{0,1:T(8,128)(2,1)S(1)}, bf16[512,128]{0,1:T(8,128)(2,1)S(1)}, u32[]{:S(2)}, u32[]{:S(2)}) collective-permute-start(bf16[512,128]{0,1:T(8,128)(2,1)S(1)} %maximum_select_fusion.4), channel_id=1, source_target_pairs={{0,2},{2,0},{1,3},{3,1},{4,6},{6,4},{5,7},{7,5},{8,10},{10,8},{9,1... | collective-permute-start | bytes 393224 | tf_op jit(solution)/shard_map/ppermute | solution.py:23
  114.4 23.5 %collective-permute-start.13 = (bf16[512,256]{0,1:T(8,128)(2,1)S(1)}, bf16[512,256]{0,1:T(8,128)(2,1)}, u32[]{:S(2)}, u32[]{:S(2)}) collective-permute-start(bf16[512,256]{0,1:T(8,128)(2,1)S(1)} %maximum_select_fusion.3), channel_id=1, source_target_pairs={{0,4},{4,0},{1,5},{5,1},{2,6},{6,2},{3,7},{7,3},{8,12},{12,8},{9,1... | collective-permute-start | bytes 786440 | tf_op jit(solution)/shard_map/ppermute | solution.py:23
  120.8 38.2 %copy-start.7 = (bf16[512,256]{0,1:T(8,128)(2,1)}, bf16[512,256]{0,1:T(8,128)(2,1)S(1)}, u32[]{:S(2)}) copy-start(bf16[512,256]{0,1:T(8,128)(2,1)S(1)} %maximum_select_fusion.2) | copy-start | bytes 786436
  120.8 38.2 %collective-permute-start.10 = (bf16[512,256]{0,1:T(8,128)(2,1)S(1)}, bf16[512,256]{0,1:T(8,128)(2,1)}, u32[]{:S(2)}, u32[]{:S(2)}) collective-permute-start(bf16[512,256]{0,1:T(8,128)(2,1)S(1)} %maximum_select_fusion.2), channel_id=1, source_target_pairs={{0,4},{4,0},{1,5},{5,1},{2,6},{6,2},{3,7},{7,3},{8,12},{12,8},{9,1... | collective-permute-start | bytes 786440 | tf_op jit(solution)/shard_map/ppermute | solution.py:23
  141.8 104.9 %collective-permute-start.5 = (f32[512,256]{0,1:T(8,128)}, f32[512,256]{0,1:T(8,128)S(1)}, u32[]{:S(2)}, u32[]{:S(2)}) collective-permute-start(f32[512,256]{0,1:T(8,128)} %constant_dynamic-slice_fusion.2), channel_id=1, source_target_pairs={{0,4},{4,0},{1,5},{5,1},{2,6},{6,2},{3,7},{7,3},{8,12},{12,8},{9,1... | collective-permute-start | bytes 1572872 | tf_op jit(solution)/shard_map/ppermute | solution.py:23
  144.5 39.5 %all-to-all-start.5 = ((f32[128,1,4]{2,1,0:T(1,128)}), f32[128,1,4]{2,1,0:T(1,128)S(1)}, u32[]{:S(2)}, u32[]{:S(2)}) async-start(f32[128,1,4]{2,1,0:T(1,128)} %bitcast.31), calls=%async_computation.5 | async-start | bytes 131072 | tf_op jit(solution)/shard_map/all_to_all | solution.py:104
  161.0 80.9 %copy-start.4 = (bf16[512,896]{1,0:T(8,128)(2,1)S(1)}, bf16[512,896]{1,0:T(8,128)(2,1)}, u32[]{:S(2)}) copy-start(bf16[512,896]{1,0:T(8,128)(2,1)} %all_to_all.39) | copy-start | bytes 2752516
  162.6 86.7 %collective-permute-start.1 = (f32[512,256]{0,1:T(8,128)}, f32[512,256]{0,1:T(8,128)}, u32[]{:S(2)}, u32[]{:S(2)}) collective-permute-start(f32[512,256]{0,1:T(8,128)} %constant_dynamic-slice_fusion.5), channel_id=1, source_target_pairs={{0,4},{4,0},{1,5},{5,1},{2,6},{6,2},{3,7},{7,3},{8,12},{12,8},{9,1... | collective-permute-start | bytes 1572872 | tf_op jit(solution)/shard_map/ppermute | solution.py:23
  184.0 19.7 %all-to-all-start.4 = ((f32[128,1,4]{2,1,0:T(1,128)}), f32[128,1,4]{2,1,0:T(1,128)S(1)}, u32[]{:S(2)}, u32[]{:S(2)}) async-start(f32[128,1,4]{2,1,0:T(1,128)} %bitcast.27), calls=%async_computation.4 | async-start | bytes 131072 | tf_op jit(solution)/shard_map/all_to_all | solution.py:104
  207.0 17.3 %all-to-all-start.2 = ((bf16[128,4,1]{1,2,0:T(2,128)(2,1)}), bf16[128,4,1]{1,2,0:T(2,128)(2,1)S(1)}, u32[]{:S(2)}, u32[]{:S(2)}) async-start(bf16[128,4,1]{1,2,0:T(2,128)(2,1)} %copy.64), calls=%async_computation.2 | async-start | bytes 131072 | tf_op jit(solution)/shard_map/all_to_all | solution.py:72
  224.4 17.3 %all-to-all-start = ((bf16[128,4,1]{1,2,0:T(2,128)(2,1)}), bf16[128,4,1]{1,2,0:T(2,128)(2,1)S(1)}, u32[]{:S(2)}, u32[]{:S(2)}) async-start(bf16[128,4,1]{1,2,0:T(2,128)(2,1)} %copy.58), calls=%async_computation | async-start | bytes 131072 | tf_op jit(solution)/shard_map/all_to_all | solution.py:72
  246.9 9.2 %collective-permute-start.6 = (f32[512,128]{0,1:T(8,128)S(1)}, f32[512,128]{0,1:T(8,128)S(1)}, u32[]{:S(2)}, u32[]{:S(2)}) collective-permute-start(f32[512,128]{0,1:T(8,128)S(1)} %constant_dynamic-slice_fusion.1), channel_id=1, source_target_pairs={{0,2},{2,0},{1,3},{3,1},{4,6},{6,4},{5,7},{7,5},{8,10},{10,8},{9,1... | collective-permute-start | bytes 786440 | tf_op jit(solution)/shard_map/ppermute | solution.py:23
  250.5 11.2 %collective-permute-start.2 = (f32[512,128]{0,1:T(8,128)S(1)}, f32[512,128]{0,1:T(8,128)S(1)}, u32[]{:S(2)}, u32[]{:S(2)}) collective-permute-start(f32[512,128]{0,1:T(8,128)S(1)} %constant_dynamic-slice_fusion.4), channel_id=1, source_target_pairs={{0,2},{2,0},{1,3},{3,1},{4,6},{6,4},{5,7},{7,5},{8,10},{10,8},{9,1... | collective-permute-start | bytes 786440 | tf_op jit(solution)/shard_map/ppermute | solution.py:23
  256.1 8.9 %collective-permute-start.7 = (f32[512,64]{0,1:T(8,128)S(1)}, f32[512,64]{0,1:T(8,128)S(1)}, u32[]{:S(2)}, u32[]{:S(2)}) collective-permute-start(f32[512,64]{0,1:T(8,128)S(1)} %constant_dynamic-slice_fusion), channel_id=1, source_target_pairs={{0,1},{1,0},{2,3},{3,2},{4,5},{5,4},{6,7},{7,6},{8,9},{9,8},{10,11... | collective-permute-start | bytes 393224 | tf_op jit(solution)/shard_map/ppermute | solution.py:23
  261.8 4.3 %collective-permute-start.3 = (f32[512,64]{0,1:T(8,128)S(1)}, f32[512,64]{0,1:T(8,128)S(1)}, u32[]{:S(2)}, u32[]{:S(2)}) collective-permute-start(f32[512,64]{0,1:T(8,128)S(1)} %constant_dynamic-slice_fusion.3), channel_id=1, source_target_pairs={{0,1},{1,0},{2,3},{3,2},{4,5},{5,4},{6,7},{7,6},{8,9},{9,8},{10,11... | collective-permute-start | bytes 393224 | tf_op jit(solution)/shard_map/ppermute | solution.py:23
  (9 other events, 99.5 us)
where the time goes:
time: 268 us; the launch traced here: 267 us
  waiting for transfers between devices  122 us (46%)
  starting transfers between devices  109 us (41%)
  local copies, waits for them, and re-layouts  15.3 us (6%)
  matrix products  11.8 us (4%)
  other arithmetic  7.73 us (3%)
    ppermute x2, waiting for transfers between devices, passed_along(): lax.ppermute(shard, axis, [(i, (i + by) % peers) for i in range(peers)])  40.6 us
    ppermute x12, starting transfers between devices, swapped(): return lax.ppermute(block, axis, route)  37.2 us
    all_to_all x2, starting transfers between devices, body(): lax.all_to_all(outgoing, 'expert', split_axis=0, concat_axis=0, tiled=True)  34.4 us
    ppermute x12, waiting for transfers between devices, swapped(): return lax.ppermute(block, axis, route)  32.1 us
    all_to_all x2, waiting for transfers between devices, body(): lax.all_to_all(score_block, 'expert', split_axis=0, concat_axis=0, tiled=...  28 us
    all_to_all x2, starting transfers between devices, body(): lax.all_to_all(score_block, 'expert', split_axis=0, concat_axis=0, tiled=...  21.6 us
    all_to_all x2, waiting for transfers between devices, body(): lax.all_to_all(gate_out, 'expert', split_axis=0, concat_axis=0, tiled=True)  19.1 us
    all_to_all x2, starting transfers between devices, body(): lax.all_to_all(gate_out, 'expert', split_axis=0, concat_axis=0, tiled=True)  11.3 us
  transfers between devices with their start and end apart: 20, of which 12 were waited for; matrix products, arithmetic and copies ran while one was open for 9% of the time, Pallas kernels for 0%

commit v1 on v0

v1 whole, which is shorter than its diff:
```python
import jax
import jax.numpy as jnp
from jax import lax
from jax.experimental import pallas as pl
from jax.experimental.pallas import tpu as pltpu
from jax.sharding import PartitionSpec as P

MICRO = 2
CAP = 4
UNIT = MICRO * CAP
ZSIDE = 8
ROW = 2 * ZSIDE
LINE = ZSIDE // 2
MESH = pl.DeviceIdType.MESH
F32 = jnp.float32
BF16 = jnp.bfloat16


def fetched(source, target, sem):
    return pltpu.make_async_copy(source, target, sem)


def arrived(block, sem):
    pltpu.make_async_copy(block, block, sem).wait()


def relay_kernel(
    sides,
    ids_ref,
    gates_ref,
    rows_hbm,
    weight_hbm,
    saved_ref,
    hidden_out,
    down_out,
    gate_out,
    rows,
    weight,
    pick_out,
    pick_in,
    row_out,
    row_in,
    disp,
    saved_all,
    scaled,
    part,
    part_in,
    peer_out,
    peer_in,
    gate_src,
    gate_row,
    gate_mid,
    gate_all,
    score_src,
    score_row,
    score_mid,
    score_all,
    load_sem,
    pick_sem,
    hop_send,
    hop_recv,
    row_send,
    row_recv,
    side_send,
    side_recv,
    saved_send,
    saved_recv,
    twin_sem,
    part_send,
    part_recv,
    peer_send,
    peer_recv,
    small_send,
    small_recv,
):
    pipes, yside = sides
    experts = yside // 2
    rounds = yside // 2
    tokens = ids_ref.shape[1]
    tok_dev = tokens // MICRO
    lanes = ROW * UNIT
    slots = saved_ref.shape[0] // MICRO
    hid = saved_ref.shape[1]
    fcols = weight.shape[1]
    pipe = lax.axis_index("pipe")
    place = lax.axis_index("expert")
    y = place // ROW
    zc = place % ROW
    z = zc // 2
    core = zc % 2
    z_line = z % LINE
    z_base = z - z_line
    before = lax.rem(pipe + pipes - 1, pipes)
    after = lax.rem(pipe + 1, pipes)
    expert = y // 2

    def remote(source, target, send, recv, where, section=pipe):
        return pltpu.make_async_remote_copy(
            src_ref=source,
            dst_ref=target,
            send_sem=send,
            recv_sem=recv,
            device_id=(section, where),
            device_id_type=MESH,
        )

    load_rows = fetched(rows_hbm, rows, load_sem.at[0])
    load_rows.start()
    load_weight = fetched(weight_hbm, weight, load_sem.at[1])
    load_weight.start()

    ids = ids_ref[...]
    gates = gates_ref[...]
    first = lax.broadcasted_iota(jnp.int32, (tokens, tokens), 0)
    second = lax.broadcasted_iota(jnp.int32, (tokens, tokens), 1)
    earlier = ((first < second) & (first // tok_dev == second // tok_dev)).astype(F32).astype(BF16)
    hits = []
    gate_tok = []
    for number in range(experts):
        named = ids == number
        hit = jnp.max(jnp.where(named, 1.0, 0.0), axis=0, keepdims=True)
        hits.append(jnp.broadcast_to(hit, (UNIT, tokens)))
        picked = jnp.sum(jnp.where(named, gates, 0.0), axis=0, keepdims=True)
        gate_tok.append(jnp.broadcast_to(picked, (UNIT, tokens)))
    hits = jnp.concatenate(hits, axis=0)
    gate_tok = jnp.concatenate(gate_tok, axis=0)
    rank = jnp.dot(hits.astype(BF16), earlier, preferred_element_type=F32)
    unit_row = lax.broadcasted_iota(jnp.int32, (experts * UNIT, tokens), 0) % UNIT
    token = lax.broadcasted_iota(jnp.int32, (experts * UNIT, tokens), 1)
    pick = jnp.where(
        (rank == (unit_row % CAP).astype(F32)) & (token // tok_dev == unit_row // CAP), hits, 0.0
    )
    pick_out[...] = pick.astype(BF16)
    send_pick = remote(pick_out, pick_in, pick_sem.at[0], pick_sem.at[1], place, after)
    send_pick.start()

    def row_cast(source, target, kind):
        own = fetched(source, target.at[zc], small_recv.at[kind])
        own.start()

        @pl.loop(1, ROW)
        def _(offset):
            peer = lax.rem(zc + offset, ROW)
            remote(
                source, target.at[zc], small_send.at[kind], small_recv.at[kind], y * ROW + peer
            ).start()

    def column_cast(source, target, kind):
        own = fetched(source, target.at[y], small_recv.at[kind])
        own.start()

        @pl.loop(1, yside)
        def _(offset):
            peer = lax.rem(y + offset, yside)
            remote(
                source, target.at[y], small_send.at[kind], small_recv.at[kind], peer * ROW + zc
            ).start()

    slot_row = lax.broadcasted_iota(jnp.int32, (experts * UNIT, lanes), 0) % UNIT
    slot_lane = lax.broadcasted_iota(jnp.int32, (experts * UNIT, lanes), 1)
    mine = slot_lane == zc * UNIT + slot_row
    gate_slot = jnp.sum(pick * gate_tok, axis=1, keepdims=True).astype(BF16).astype(F32)
    gate_lane = jnp.where(mine, gate_slot, 0.0)
    pieces = [
        jnp.sum(gate_lane[number * UNIT : (number + 1) * UNIT], axis=0, keepdims=True)
        for number in range(experts)
    ]
    pieces += [jnp.zeros((8 - experts, lanes), F32)]
    gate_src[...] = jnp.concatenate(pieces, axis=0)
    row_cast(gate_src, gate_row, 0)

    line_row = lax.broadcasted_iota(jnp.int32, (lanes, lanes), 0)
    line_col = lax.broadcasted_iota(jnp.int32, (lanes, lanes), 1)
    per_micro = ROW * CAP
    micro_of = line_row // per_micro
    within = line_row % per_micro
    order = (line_col == (within // CAP) * UNIT + micro_of * CAP + within % CAP).astype(F32).astype(BF16)
    for number in range(yside):
        block = jnp.concatenate(
            [
                saved_ref[micro * slots + number * per_micro : micro * slots + (number + 1) * per_micro, :]
                for micro in range(MICRO)
            ],
            axis=0,
        )
        turned = lax.dot_general(
            block, order, (((0,), (0,)), ((), ())), preferred_element_type=F32
        )
        saved_all[core, z_line, number] = turned.astype(BF16)
    for offset in range(1, LINE):
        target = z_base + lax.rem(z_line + offset, LINE)
        remote(
            saved_all.at[core, z_line],
            saved_all.at[core, z_line],
            saved_send.at[offset],
            saved_recv.at[offset],
            y * ROW + target * 2 + core,
        ).start()

    load_rows.wait()
    send_pick.wait_recv()
    chosen = pick_in[...]
    for block in range(2 * LINE):
        taken = jnp.dot(
            chosen, rows[:, block * fcols : (block + 1) * fcols], preferred_element_type=F32
        )
        for number in range(experts):
            row_out[number, block] = taken[number * UNIT : (number + 1) * UNIT].astype(BF16)
    hops = []
    for turn in range(rounds):
        even = (y + turn) % 2 == 0
        y_to = lax.rem(jnp.where(even, y + turn, y + yside - turn), yside)
        hop = remote(
            row_out.at[y_to // 2],
            row_in.at[turn],
            hop_send.at[turn],
            hop_recv.at[turn],
            y_to * ROW + zc,
            before,
        )
        hop.start()
        hops.append(hop)

    def source_of(y_at, turn):
        return lax.rem(jnp.where(y_at % 2 == 0, y_at + yside - turn, y_at + turn), yside)

    def spread(turn):
        hops[turn].wait_recv()
        slot = source_of(y, turn) * ROW + zc
        own = fetched(
            row_in.at[turn, z_line * 2 + core], disp.at[slot], row_recv.at[turn]
        )
        own.start()

        @pl.loop(1, ROW)
        def _(offset):
            peer = lax.rem(zc + offset, ROW)
            block = ((peer // 2) % LINE) * 2 + peer % 2
            remote(
                row_in.at[turn, block],
                disp.at[slot],
                row_send.at[turn],
                row_recv.at[turn],
                y * ROW + peer,
            ).start()

    partner = jnp.where(y % 2 == 0, y + 1, y - 1)
    twin = y * ROW + z * 2 + (1 - core)
    shares = []

    def receive(step, owned, turn):
        if owned:
            source = source_of(y, turn)
            region = disp.at[pl.ds(source * ROW, ROW)]
            arrived(region, row_recv.at[turn])
            remote(
                region, region, side_send.at[turn], side_recv.at[turn], partner * ROW + zc
            ).start()
        else:
            source = source_of(partner, turn)
            region = disp.at[pl.ds(source * ROW, ROW)]
            arrived(region, side_recv.at[turn])
        value = disp[pl.ds(source * ROW, ROW)].reshape(ROW * UNIT, fcols)
        product = lax.dot_general(
            weight[...], value, (((1,), (1,)), ((), ())), preferred_element_type=F32
        )
        part[step] = product.reshape(LINE, 2, hid, lanes)
        share = remote(
            part.at[step, :, 1 - core],
            part_in.at[step],
            part_send.at[step],
            part_recv.at[step],
            twin,
        )
        share.start()
        shares.append((source, share))

    def pass_on(step):
        shares[step][1].wait_recv()
        peer_out[step] = (part[step, :, core] + part_in[step]).astype(BF16)
        for offset in range(1, LINE):
            target = lax.rem(z_line + offset, LINE)
            remote(
                peer_out.at[step, target],
                peer_in.at[step, offset],
                peer_send.at[step, offset],
                peer_recv.at[step, offset],
                y * ROW + (z_base + target) * 2 + core,
            ).start()

    def finish(step):
        source = shares[step][0]
        for offset in range(1, LINE):
            arrived(peer_in.at[step, offset], peer_recv.at[step, offset])
        total = part[step, z_line, core] + part_in[step, z_line]
        for offset in range(1, LINE):
            total = total + peer_in[step, offset].astype(F32)
        kept = saved_all[core, z_line, source].astype(F32)
        score_src[pl.ds(source, 1), :] = jnp.sum(total * kept, axis=0, keepdims=True)
        gated = (gate_all[source, pl.ds(expert, 1), :] * total).astype(BF16)
        turned = lax.dot_general(
            order, gated, (((1,), (1,)), ((), ())), preferred_element_type=F32
        ).astype(BF16)
        for micro in range(MICRO):
            start = pl.multiple_of(micro * slots + source * per_micro, per_micro)
            hidden_out[pl.ds(start, per_micro), :] = turned[
                micro * per_micro : (micro + 1) * per_micro
            ]

    plan = []
    for turn in range(rounds):
        plan.append((True, turn))
        if turn >= 1:
            plan.append((False, turn - 1))
    plan.append((False, rounds - 1))

    spread(0)
    arrived(gate_row, small_recv.at[0])
    summed = gate_row[0]
    for number in range(1, ROW):
        summed = summed + gate_row[number]
    gate_mid[...] = summed
    column_cast(gate_mid, gate_all, 1)
    load_weight.wait()
    issued = 1
    for step, (owned, turn) in enumerate(plan):
        while issued < rounds and issued <= step + 1:
            spread(issued)
            issued += 1
        receive(step, owned, turn)
        if step >= 1:
            pass_on(step - 1)
        if step == 1:
            arrived(gate_all, small_recv.at[1])
        if step >= 2:
            finish(step - 2)
    last = len(plan) - 1
    pass_on(last)
    for offset in range(1, LINE):
        origin = lax.rem(z_line + LINE - offset, LINE)
        arrived(saved_all.at[core, origin], saved_recv.at[offset])
    share_saved = remote(
        saved_all.at[core], saved_all.at[core], twin_sem.at[0], twin_sem.at[1], twin
    )
    share_saved.start()
    if last >= 1:
        finish(last - 1)
    finish(last)
    row_cast(score_src, score_row, 2)
    arrived(saved_all.at[1 - core], twin_sem.at[1])
    for number in range(yside):
        scale = gate_all[number, pl.ds(expert, 1), :]
        for line in range(LINE):
            for side in range(2):
                at = (line * 2 + side) * hid
                scaled[at : at + hid, number * lanes : (number + 1) * lanes] = (
                    saved_all[side, line, number].astype(F32) * scale
                ).astype(BF16)
    arrived(score_row, small_recv.at[2])
    summed = score_row[0]
    for number in range(1, ROW):
        summed = summed + score_row[number]
    score_mid[...] = summed
    column_cast(score_mid, score_all, 3)
    width = 256
    for start in range(0, fcols, width):
        stop = min(start + width, fcols)
        value = disp[:, :, start:stop].reshape(yside * ROW * UNIT, stop - start)
        down_out[:, start:stop] = jnp.dot(
            scaled[...], value, preferred_element_type=F32
        ).astype(BF16)
    arrived(score_all, small_recv.at[3])
    lines = []
    for number in range(experts):
        both = score_all[2 * number, pl.ds(y, 1), :] + score_all[2 * number + 1, pl.ds(y, 1), :]
        lines.append(jnp.broadcast_to(both, (UNIT, lanes)))
    slot_score = jnp.sum(
        jnp.where(mine, jnp.concatenate(lines, axis=0), 0.0), axis=1, keepdims=True
    )
    spread_score = pick * slot_score
    result = jnp.zeros(ids.shape, F32)
    for number in range(experts):
        by_token = jnp.sum(
            spread_score[number * UNIT : (number + 1) * UNIT], axis=0, keepdims=True
        )
        result = result + jnp.where(ids == number, by_token, 0.0)
    gate_out[...] = result

    send_pick.wait_send()
    for turn in range(rounds):
        hops[turn].wait_send()
        arrived(disp.at[pl.ds(0, ROW - 1)], row_send.at[turn])
        arrived(disp.at[pl.ds(0, ROW)], side_send.at[turn])
    for offset in range(1, LINE):
        arrived(saved_all.at[0, 0], saved_send.at[offset])
    share_saved.wait_send()
    for step in range(len(plan)):
        shares[step][1].wait_send()
        for offset in range(1, LINE):
            arrived(peer_out.at[step, 0], peer_send.at[step, offset])
    for kind, count, block in (
        (0, ROW - 1, gate_row),
        (1, yside - 1, gate_all),
        (2, ROW - 1, score_row),
        (3, yside - 1, score_all),
    ):
        arrived(block.at[pl.ds(0, count)], small_send.at[kind])


def body(out_grad, expert_ids, gate_values, down_tiles, hidden_saved):
    pipes = lax.axis_size("pipe")
    devices = lax.axis_size("expert")
    yside = devices // ROW
    rounds = yside // 2
    steps = yside
    experts = yside // 2
    _, micro, tok_dev, width = out_grad.shape
    _, _, tile_rows, tile_cols = down_tiles.shape
    _, _, slots, hid = hidden_saved.shape
    topk = expert_ids.shape[-1]
    tokens = micro * tok_dev
    lanes = ROW * UNIT
    ids = expert_ids.reshape(tokens, topk).T
    gates = gate_values.reshape(tokens, topk).T
    vmem = pl.BlockSpec(memory_space=pltpu.VMEM)
    anywhere = pl.BlockSpec(memory_space=pl.ANY)
    dma = pltpu.SemaphoreType.DMA
    hidden_grad, down_grad, gate_grad = pl.pallas_call(
        lambda *refs: relay_kernel((pipes, yside), *refs),
        out_shape=(
            jax.ShapeDtypeStruct((micro * slots, hid), BF16),
            jax.ShapeDtypeStruct((tile_rows, tile_cols), BF16),
            jax.ShapeDtypeStruct((topk, tokens), F32),
        ),
        in_specs=[vmem, vmem, anywhere, anywhere, vmem],
        out_specs=(vmem, vmem, vmem),
        scratch_shapes=[
            pltpu.VMEM((tokens, width), BF16),
            pltpu.VMEM((tile_rows, tile_cols), BF16),
            pltpu.VMEM((experts * UNIT, tokens), BF16),
            pltpu.VMEM((experts * UNIT, tokens), BF16),
            pltpu.VMEM((experts, 2 * LINE, UNIT, tile_cols), BF16),
            pltpu.VMEM((rounds, 2 * LINE, UNIT, tile_cols), BF16),
            pltpu.VMEM((devices, UNIT, tile_cols), BF16),
            pltpu.VMEM((2, LINE, yside, hid, lanes), BF16),
            pltpu.VMEM((tile_rows, yside * lanes), BF16),
            pltpu.VMEM((steps, LINE, 2, hid, lanes), F32),
            pltpu.VMEM((steps, LINE, hid, lanes), F32),
            pltpu.VMEM((steps, LINE, hid, lanes), BF16),
            pltpu.VMEM((steps, LINE, hid, lanes), BF16),
            pltpu.VMEM((8, lanes), F32),
            pltpu.VMEM((ROW, 8, lanes), F32),
            pltpu.VMEM((8, lanes), F32),
            pltpu.VMEM((yside, 8, lanes), F32),
            pltpu.VMEM((yside, lanes), F32),
            pltpu.VMEM((ROW, yside, lanes), F32),
            pltpu.VMEM((yside, lanes), F32),
            pltpu.VMEM((yside, yside, lanes), F32),
            dma((2,)),
            dma((2,)),
            dma((rounds,)),
            dma((rounds,)),
            dma((rounds,)),
            dma((rounds,)),
            dma((rounds,)),
            dma((rounds,)),
            dma((LINE,)),
            dma((LINE,)),
            dma((2,)),
            dma((steps,)),
            dma((steps,)),
            dma((steps, LINE)),
            dma((steps, LINE)),
            dma((4,)),
            dma((4,)),
        ],
        compiler_params=pltpu.CompilerParams(
            has_side_effects=True, vmem_limit_bytes=40 * 2**20
        ),
        name="relay",
    )(
        ids,
        gates,
        out_grad.reshape(tokens, width),
        down_tiles.reshape(tile_rows, tile_cols),
        hidden_saved.reshape(micro * slots, hid),
    )
    return (
        hidden_grad.reshape(1, micro, slots, hid),
        down_grad.reshape(1, 1, tile_rows, tile_cols),
        gate_grad.T.reshape(1, micro, tok_dev, topk),
    )


def solution(mesh):
    return jax.shard_map(
        body,
        mesh=mesh,
        in_specs=(
            P("pipe", None, "expert", None),
            P("pipe", None, "expert", None),
            P("pipe", None, "expert", None),
            P("pipe", "expert", None, None),
            P("pipe", None, None, "expert"),
        ),
        out_specs=(
            P("pipe", None, None, "expert"),
            P("pipe", "expert", None, None),
            P("pipe", None, "expert", None),
        ),
        check_vma=False,
    )
```

time: 268 us -> 98.7 us (0.37)
  waiting for transfers between devices: 122 us -> 0 us
  starting transfers between devices: 109 us -> 0 us
  Pallas kernels: 0 us -> 89.5 us
  matrix products: 11.8 us -> 0 us
  other arithmetic: 7.73 us -> 0 us
  local copies, waits for them, and re-layouts: 15.3 us -> 7.7 us
    pallas_call x0 -> x1, Pallas kernels: none -> 89.5 us  [body(): pl.pallas_call(lambda *refs: relay_kernel((pipes, yside), *refs), out_sha...]
    ppermute x14 -> x0, waiting for transfers between devices: 72.7 us -> none  [the longest x2 40.6 us: passed_along(): lax.ppermute(shard, axis, [(i, (i + by) % peers) for i in range(peers)])]
    all_to_all x6 -> x0, starting transfers between devices: 67.3 us -> none  [the longest x2 34.4 us: body(): lax.all_to_all(outgoing, 'expert', split_axis=0, concat_axis=0, tiled=True)]
    all_to_all x6 -> x0, waiting for transfers between devices: 49.2 us -> none  [the longest x2 28 us: body(): lax.all_to_all(score_block, 'expert', split_axis=0, concat_axis=0, tiled=...]
    ppermute x14 -> x0, starting transfers between devices: 41.5 us -> none  [the longest x12 37.2 us: swapped(): return lax.ppermute(block, axis, route)]
    dot_general x6 -> x0, matrix products: 11.8 us -> none  [the longest x2 4.75 us: body(): lax.dot_general(scaled, received, (((0,), (0,)), ((), ())), preferred_ele...]
    unnamed x28 -> x10, local copies, waits for them, and re-layouts: 1.1 us -> 7.46 us
    all_to_all x4 -> x0, local copies, waits for them, and re-layouts: 3.76 us -> none  [the longest x2 2.3 us: body(): lax.all_to_all(outgoing, 'expert', split_axis=0, concat_axis=0, tiled=True)]
  transfers between devices with their start and end apart: 20 -> 0, of which waited for: 12 -> 0; matrix products, arithmetic and copies ran while one was open for 9% -> 0% of each run, Pallas kernels for 0% -> 0%
where the time goes in v1:
time: 98.7 us; the launch traced here: 97.9 us
  Pallas kernels  89.5 us (91%)
  local copies, waits for them, and re-layouts  7.7 us (8%)
    pallas_call x1, Pallas kernels, body(): pl.pallas_call(lambda *refs: relay_kernel((pipes, yside), *refs), out_sha...  89.5 us
    unnamed x10, local copies, waits for them, and re-layouts  7.46 us

profile of v1, /device:TPU:7, one launch (start us, length us, event | category | flops | bytes accessed | tf_op | source)
XLA Modules:
  0.0 97.9 jit_solution(5657823287381000639)
XLA Ops:
  0.6 0.7 copy.8
  1.3 0.1 reshape.30
  1.4 0.7 copy.9
  2.1 0.1 reshape.31
  2.2 1.1 %copy.10 = bf16[1,2,512,64]{3,2,1,0:T(8,128)(2,1)S(1)} copy(bf16[1,2,512,64]{2,3,1,0:T(8,128)(2,1)} %param.9) | data formatting | bytes 262144 | tf_op args[4]
  3.3 0.0 copy-start
  3.3 1.5 %copy-done = bf16[1,2,64,7168]{3,2,1,0:T(8,128)(2,1)S(1)} copy-done((bf16[1,2,64,7168]{3,2,1,0:T(8,128)(2,1)S(1)}, bf16[1,2,64,7168]{3,2,1,0:T(8,128)(2,1)}, u32[]{:S(2)}) %copy-start) | copy-done | bytes 1835032
  4.8 0.0 copy-start.1
  4.8 1.2 %copy-done.1 = bf16[1,1,512,896]{3,2,1,0:T(8,128)(2,1)S(1)} copy-done((bf16[1,1,512,896]{3,2,1,0:T(8,128)(2,1)S(1)}, bf16[1,1,512,896]{3,2,1,0:T(8,128)(2,1)}, u32[]{:S(2)}) %copy-start.1) | copy-done | bytes 917528
  6.0 89.5 %relay.1 = (bf16[1024,64]{1,0:T(8,128)(2,1)S(1)}, bf16[512,896]{1,0:T(8,128)(2,1)S(1)}, f32[8,128]{1,0:T(8,128)S(1)}) custom-call(s32[8,128]{1,0:T(8,128)S(1)} %bitcast.19, f32[8,128]{1,0:T(8,128)S(1)} %bitcast.20, bf16[128,7168]{1,0:T(8,128)(2,1)S(1)} %bitcast.14, bf16[512,896]{1,0:T(8,128)(2,1)S(1)} %bitcast.17, bf16[1024,64]{1,0:T(8,128)(2,1)S(1)} %bitcast.15), custom_call_target="tpu_custom_call" | custom-call | tf_op jit(solution)/shard_map/relay/pallas_call | solution.py:428
  95.5 0.8 copy.11
  96.3 0.1 reshape.37
  96.3 0.6 copy.12
  97.0 0.9 copy.14
Async XLA Ops:
  3.3 1.5 %copy-start = (bf16[1,2,64,7168]{3,2,1,0:T(8,128)(2,1)S(1)}, bf16[1,2,64,7168]{3,2,1,0:T(8,128)(2,1)}, u32[]{:S(2)}) copy-start(bf16[1,2,64,7168]{3,2,1,0:T(8,128)(2,1)} %param.5) | copy-start | bytes 5505028
  4.8 1.2 %copy-start.1 = (bf16[1,1,512,896]{3,2,1,0:T(8,128)(2,1)S(1)}, bf16[1,1,512,896]{3,2,1,0:T(8,128)(2,1)}, u32[]{:S(2)}) copy-start(bf16[1,1,512,896]{3,2,1,0:T(8,128)(2,1)} %param.8) | copy-start | bytes 2752516

commit v2 on v1

--- a/solution.py
+++ b/solution.py
@@ -30,19 +30,20 @@
     gates_ref,
     rows_hbm,
     weight_hbm,
-    saved_ref,
+    saved_hbm,
     hidden_out,
     down_out,
     gate_out,
     rows,
     weight,
+    saved,
     pick_out,
     pick_in,
     row_out,
     row_in,
     disp,
     saved_all,
-    scaled,
+    total,
     part,
     part_in,
     peer_out,
@@ -52,9 +53,10 @@
     gate_mid,
     gate_all,
     score_src,
+    score_col,
+    score_mid,
     score_row,
-    score_mid,
-    score_all,
+    turned_all,
     load_sem,
     pick_sem,
     hop_send,
@@ -76,11 +78,10 @@
     pipes, yside = sides
     experts = yside // 2
     rounds = yside // 2
-    tokens = ids_ref.shape[1]
-    tok_dev = tokens // MICRO
+    tok_dev = ids_ref.shape[2]
+    tokens = tok_dev * MICRO
     lanes = ROW * UNIT
-    slots = saved_ref.shape[0] // MICRO
-    hid = saved_ref.shape[1]
+    hid = saved.shape[1]
     fcols = weight.shape[1]
     pipe = lax.axis_index("pipe")
     place = lax.axis_index("expert")
@@ -104,13 +105,31 @@
             device_id_type=MESH,
         )
 
+    def source_of(y_at, turn):
+        return lax.rem(jnp.where(y_at % 2 == 0, y_at + yside - turn, y_at + turn), yside)
+
+    barrier = pltpu.get_barrier_semaphore()
+
+    def greet(where, section=pipe):
+        pl.semaphore_signal(barrier, inc=1, device_id=(section, where), device_id_type=MESH)
+
+    greet(place, before)
+    for turn in range(rounds):
+        greet(source_of(y, turn) * ROW + zc, after)
+    for offset in range(1, ROW):
+        greet(y * ROW + lax.rem(zc + offset, ROW))
+    for offset in range(1, yside):
+        greet(lax.rem(y + offset, yside) * ROW + zc)
+
     load_rows = fetched(rows_hbm, rows, load_sem.at[0])
     load_rows.start()
+    load_saved = fetched(saved_hbm, saved, load_sem.at[2])
+    load_saved.start()
     load_weight = fetched(weight_hbm, weight, load_sem.at[1])
     load_weight.start()
 
-    ids = ids_ref[...]
-    gates = gates_ref[...]
+    ids = jnp.concatenate([ids_ref[micro] for micro in range(MICRO)], axis=1)
+    gates = jnp.concatenate([gates_ref[micro] for micro in range(MICRO)], axis=1)
     first = lax.broadcasted_iota(jnp.int32, (tokens, tokens), 0)
     second = lax.broadcasted_iota(jnp.int32, (tokens, tokens), 1)
     earlier = ((first < second) & (first // tok_dev == second // tok_dev)).astype(F32).astype(BF16)
@@ -131,6 +150,7 @@
         (rank == (unit_row % CAP).astype(F32)) & (token // tok_dev == unit_row // CAP), hits, 0.0
     )
     pick_out[...] = pick.astype(BF16)
+    pl.semaphore_wait(barrier, 1 + rounds + ROW - 1 + yside - 1)
     send_pick = remote(pick_out, pick_in, pick_sem.at[0], pick_sem.at[1], place, after)
     send_pick.start()
 
@@ -175,18 +195,18 @@
     micro_of = line_row // per_micro
     within = line_row % per_micro
     order = (line_col == (within // CAP) * UNIT + micro_of * CAP + within % CAP).astype(F32).astype(BF16)
+    load_saved.wait()
     for number in range(yside):
         block = jnp.concatenate(
             [
-                saved_ref[micro * slots + number * per_micro : micro * slots + (number + 1) * per_micro, :]
+                saved[micro, :, number * per_micro : (number + 1) * per_micro]
                 for micro in range(MICRO)
             ],
-            axis=0,
-        )
-        turned = lax.dot_general(
-            block, order, (((0,), (0,)), ((), ())), preferred_element_type=F32
-        )
-        saved_all[core, z_line, number] = turned.astype(BF16)
+            axis=1,
+        )
+        saved_all[core, z_line, number] = jnp.dot(
+            block, order, preferred_element_type=F32
+        ).astype(BF16)
     for offset in range(1, LINE):
         target = z_base + lax.rem(z_line + offset, LINE)
         remote(
@@ -220,9 +240,6 @@
         )
         hop.start()
         hops.append(hop)
-
-    def source_of(y_at, turn):
-        return lax.rem(jnp.where(y_at % 2 == 0, y_at + yside - turn, y_at + turn), yside)
 
     def spread(turn):
         hops[turn].wait_recv()
@@ -274,6 +291,24 @@
         )
         share.start()
         shares.append((source, share))
+        if step == 0:
+            arrived(saved_all.at[1 - core], twin_sem.at[1])
+        score = jnp.zeros((hid, lanes), F32)
+        for line in range(LINE):
+            for side in range(2):
+                at = (line * 2 + side) * hid
+                score += saved_all[side, line, source].astype(F32) * product[at : at + hid]
+        score_src[step] = jnp.sum(score, axis=0, keepdims=True)
+        if owned and turn == 0:
+            fetched(score_src.at[step], score_col.at[y], small_recv.at[2]).start()
+        else:
+            remote(
+                score_src.at[step],
+                score_col.at[y],
+                small_send.at[2],
+                small_recv.at[2],
+                source * ROW + zc,
+            ).start()
 
     def pass_on(step):
         shares[step][1].wait_recv()
@@ -292,20 +327,33 @@
         source = shares[step][0]
         for offset in range(1, LINE):
             arrived(peer_in.at[step, offset], peer_recv.at[step, offset])
-        total = part[step, z_line, core] + part_in[step, z_line]
+        whole = part[step, z_line, core] + part_in[step, z_line]
         for offset in range(1, LINE):
-            total = total + peer_in[step, offset].astype(F32)
-        kept = saved_all[core, z_line, source].astype(F32)
-        score_src[pl.ds(source, 1), :] = jnp.sum(total * kept, axis=0, keepdims=True)
-        gated = (gate_all[source, pl.ds(expert, 1), :] * total).astype(BF16)
-        turned = lax.dot_general(
-            order, gated, (((1,), (1,)), ((), ())), preferred_element_type=F32
+            whole = whole + peer_in[step, offset].astype(F32)
+        gated = (gate_all[source, pl.ds(expert, 1), :] * whole).astype(BF16)
+        turned_all[source] = lax.dot_general(
+            gated, order, (((1,), (1,)), ((), ())), preferred_element_type=F32
         ).astype(BF16)
-        for micro in range(MICRO):
-            start = pl.multiple_of(micro * slots + source * per_micro, per_micro)
-            hidden_out[pl.ds(start, per_micro), :] = turned[
-                micro * per_micro : (micro + 1) * per_micro
-            ]
+
+    def grow(step):
+        source = shares[step][0]
+        scale = gate_all[source, pl.ds(expert, 1), :]
+        left = jnp.concatenate(
+            [
+                (saved_all[side, line, source].astype(F32) * scale).astype(BF16)
+                for line in range(LINE)
+                for side in range(2)
+            ],
+            axis=0,
+        )
+        value = disp[pl.ds(source * ROW, ROW)].reshape(ROW * UNIT, fcols)
+        update = jnp.dot(left, value, preferred_element_type=F32)
+        if step > 0:
+            update = total[...] + update
+        if step < yside - 1:
+            total[...] = update
+        else:
+            down_out[...] = update.astype(BF16)
 
     plan = []
     for turn in range(rounds):
@@ -314,66 +362,57 @@
             plan.append((False, turn - 1))
     plan.append((False, rounds - 1))
 
-    spread(0)
-    arrived(gate_row, small_recv.at[0])
-    summed = gate_row[0]
-    for number in range(1, ROW):
-        summed = summed + gate_row[number]
-    gate_mid[...] = summed
-    column_cast(gate_mid, gate_all, 1)
+    for turn in range(rounds):
+        spread(turn)
+        if turn == 0:
+            arrived(gate_row, small_recv.at[0])
+            summed = gate_row[0]
+            for number in range(1, ROW):
+                summed = summed + gate_row[number]
+            gate_mid[...] = summed
+            column_cast(gate_mid, gate_all, 1)
+            for offset in range(1, LINE):
+                origin = lax.rem(z_line + LINE - offset, LINE)
+                arrived(saved_all.at[core, origin], saved_recv.at[offset])
+            share_saved = remote(
+                saved_all.at[core], saved_all.at[core], twin_sem.at[0], twin_sem.at[1], twin
+            )
+            share_saved.start()
     load_weight.wait()
-    issued = 1
     for step, (owned, turn) in enumerate(plan):
-        while issued < rounds and issued <= step + 1:
-            spread(issued)
-            issued += 1
         receive(step, owned, turn)
+        if step == 0:
+            arrived(gate_all, small_recv.at[1])
         if step >= 1:
             pass_on(step - 1)
-        if step == 1:
-            arrived(gate_all, small_recv.at[1])
+        grow(step)
         if step >= 2:
             finish(step - 2)
     last = len(plan) - 1
     pass_on(last)
-    for offset in range(1, LINE):
-        origin = lax.rem(z_line + LINE - offset, LINE)
-        arrived(saved_all.at[core, origin], saved_recv.at[offset])
-    share_saved = remote(
-        saved_all.at[core], saved_all.at[core], twin_sem.at[0], twin_sem.at[1], twin
-    )
-    share_saved.start()
+    arrived(score_col, small_recv.at[2])
+    lines = [score_col[2 * number] + score_col[2 * number + 1] for number in range(experts)]
+    lines += [jnp.zeros((8 - experts, lanes), F32)]
+    score_mid[...] = jnp.concatenate(lines, axis=0)
+    row_cast(score_mid, score_row, 3)
     if last >= 1:
         finish(last - 1)
     finish(last)
-    row_cast(score_src, score_row, 2)
-    arrived(saved_all.at[1 - core], twin_sem.at[1])
-    for number in range(yside):
-        scale = gate_all[number, pl.ds(expert, 1), :]
-        for line in range(LINE):
-            for side in range(2):
-                at = (line * 2 + side) * hid
-                scaled[at : at + hid, number * lanes : (number + 1) * lanes] = (
-                    saved_all[side, line, number].astype(F32) * scale
-                ).astype(BF16)
-    arrived(score_row, small_recv.at[2])
+    for micro in range(MICRO):
+        hidden_out[micro] = jnp.concatenate(
+            [
+                turned_all[number, :, micro * per_micro : (micro + 1) * per_micro]
+                for number in range(yside)
+            ],
+            axis=1,
+        )
+    arrived(score_row, small_recv.at[3])
     summed = score_row[0]
     for number in range(1, ROW):
         summed = summed + score_row[number]
-    score_mid[...] = summed
-    column_cast(score_mid, score_all, 3)
-    width = 256
-    for start in range(0, fcols, width):
-        stop = min(start + width, fcols)
-        value = disp[:, :, start:stop].reshape(yside * ROW * UNIT, stop - start)
-        down_out[:, start:stop] = jnp.dot(
-            scaled[...], value, preferred_element_type=F32
-        ).astype(BF16)
-    arrived(score_all, small_recv.at[3])
-    lines = []
-    for number in range(experts):
-        both = score_all[2 * number, pl.ds(y, 1), :] + score_all[2 * number + 1, pl.ds(y, 1), :]
-        lines.append(jnp.broadcast_to(both, (UNIT, lanes)))
+    lines = [
+        jnp.broadcast_to(summed[number : number + 1], (UNIT, lanes)) for number in range(experts)
+    ]
     slot_score = jnp.sum(
         jnp.where(mine, jnp.concatenate(lines, axis=0), 0.0), axis=1, keepdims=True
     )
@@ -384,7 +423,8 @@
             spread_score[number * UNIT : (number + 1) * UNIT], axis=0, keepdims=True
         )
         result = result + jnp.where(ids == number, by_token, 0.0)
-    gate_out[...] = result
+    for micro in range(MICRO):
+        gate_out[micro] = result[:, micro * tok_dev : (micro + 1) * tok_dev]
 
     send_pick.wait_send()
     for turn in range(rounds):
@@ -401,8 +441,8 @@
     for kind, count, block in (
         (0, ROW - 1, gate_row),
         (1, yside - 1, gate_all),
-        (2, ROW - 1, score_row),
-        (3, yside - 1, score_all),
+        (2, yside - 1, score_col),
+        (3, ROW - 1, score_row),
     ):
         arrived(block.at[pl.ds(0, count)], small_send.at[kind])
 
@@ -420,30 +460,32 @@
     topk = expert_ids.shape[-1]
     tokens = micro * tok_dev
     lanes = ROW * UNIT
-    ids = expert_ids.reshape(tokens, topk).T
-    gates = gate_values.reshape(tokens, topk).T
+    ids = expert_ids.transpose(0, 1, 3, 2).reshape(micro, topk, tok_dev)
+    gates = gate_values.transpose(0, 1, 3, 2).reshape(micro, topk, tok_dev)
+    saved = hidden_saved.transpose(0, 1, 3, 2).reshape(micro, hid, slots)
     vmem = pl.BlockSpec(memory_space=pltpu.VMEM)
-    anywhere = pl.BlockSpec(memory_space=pl.ANY)
+    far = pl.BlockSpec(memory_space=pltpu.HBM)
     dma = pltpu.SemaphoreType.DMA
     hidden_grad, down_grad, gate_grad = pl.pallas_call(
         lambda *refs: relay_kernel((pipes, yside), *refs),
         out_shape=(
-            jax.ShapeDtypeStruct((micro * slots, hid), BF16),
+            jax.ShapeDtypeStruct((micro, hid, slots), BF16),
             jax.ShapeDtypeStruct((tile_rows, tile_cols), BF16),
-            jax.ShapeDtypeStruct((topk, tokens), F32),
+            jax.ShapeDtypeStruct((micro, topk, tok_dev), F32),
         ),
-        in_specs=[vmem, vmem, anywhere, anywhere, vmem],
+        in_specs=[vmem, vmem, far, far, far],
         out_specs=(vmem, vmem, vmem),
         scratch_shapes=[
             pltpu.VMEM((tokens, width), BF16),
             pltpu.VMEM((tile_rows, tile_cols), BF16),
+            pltpu.VMEM((micro, hid, slots), BF16),
             pltpu.VMEM((experts * UNIT, tokens), BF16),
             pltpu.VMEM((experts * UNIT, tokens), BF16),
             pltpu.VMEM((experts, 2 * LINE, UNIT, tile_cols), BF16),
             pltpu.VMEM((rounds, 2 * LINE, UNIT, tile_cols), BF16),
             pltpu.VMEM((devices, UNIT, tile_cols), BF16),
             pltpu.VMEM((2, LINE, yside, hid, lanes), BF16),
-            pltpu.VMEM((tile_rows, yside * lanes), BF16),
+            pltpu.VMEM((tile_rows, tile_cols), F32),
             pltpu.VMEM((steps, LINE, 2, hid, lanes), F32),
             pltpu.VMEM((steps, LINE, hid, lanes), F32),
             pltpu.VMEM((steps, LINE, hid, lanes), BF16),
@@ -452,11 +494,12 @@
             pltpu.VMEM((ROW, 8, lanes), F32),
             pltpu.VMEM((8, lanes), F32),
             pltpu.VMEM((yside, 8, lanes), F32),
-            pltpu.VMEM((yside, lanes), F32),
-            pltpu.VMEM((ROW, yside, lanes), F32),
-            pltpu.VMEM((yside, lanes), F32),
-            pltpu.VMEM((yside, yside, lanes), F32),
-            dma((2,)),
+            pltpu.VMEM((yside, 1, lanes), F32),
+            pltpu.VMEM((yside, 1, lanes), F32),
+            pltpu.VMEM((8, lanes), F32),
+            pltpu.VMEM((ROW, 8, lanes), F32),
+            pltpu.VMEM((yside, hid, lanes), BF16),
+            dma((3,)),
             dma((2,)),
             dma((rounds,)),
             dma((rounds,)),
@@ -475,7 +518,7 @@
             dma((4,)),
         ],
         compiler_params=pltpu.CompilerParams(
-            has_side_effects=True, vmem_limit_bytes=40 * 2**20
+            has_side_effects=True, collective_id=0, vmem_limit_bytes=62 * 2**20
         ),
         name="relay",
     )(
@@ -483,12 +526,12 @@
         gates,
         out_grad.reshape(tokens, width),
         down_tiles.reshape(tile_rows, tile_cols),
-        hidden_saved.reshape(micro * slots, hid),
+        saved,
     )
     return (
-        hidden_grad.reshape(1, micro, slots, hid),
+        hidden_grad.reshape(1, micro, hid, slots).transpose(0, 1, 3, 2),
         down_grad.reshape(1, 1, tile_rows, tile_cols),
-        gate_grad.T.reshape(1, micro, tok_dev, topk),
+        gate_grad.reshape(1, micro, topk, tok_dev).transpose(0, 1, 3, 2),
     )
 
 

time: 98.7 us -> 80.6 us (0.82)
  Pallas kernels: 89.5 us -> 75.4 us
  local copies, waits for them, and re-layouts: 7.7 us -> 4.35 us
    pallas_call x1, Pallas kernels: 89.5 us -> 75.4 us  [body(): pl.pallas_call(lambda *refs: relay_kernel((pipes, yside), *refs), out_sha...]
    unnamed x10 -> x5, local copies, waits for them, and re-layouts: 7.46 us -> 4.35 us
where the time goes in v2:
time: 80.6 us; the launch traced here: 80.4 us
  Pallas kernels  75.4 us (94%)
  local copies, waits for them, and re-layouts  4.35 us (5%)
    pallas_call x1, Pallas kernels, body(): pl.pallas_call(lambda *refs: relay_kernel((pipes, yside), *refs), out_sha...  75.4 us
    unnamed x5, local copies, waits for them, and re-layouts  4.35 us

profile of v2, /device:TPU:7, one launch (start us, length us, event | category | flops | bytes accessed | tf_op | source)
XLA Modules:
  0.0 80.4 jit_solution(8241961569901387692)
XLA Ops:
  0.6 75.4 %relay.1 = (bf16[2,64,512]{2,1,0:T(8,128)(2,1)}, bf16[512,896]{1,0:T(8,128)(2,1)}, f32[2,8,64]{2,1,0:T(8,128)}) custom-call(s32[2,8,64]{2,1,0:T(8,128)} %bitcast.23, f32[2,8,64]{2,1,0:T(8,128)} %bitcast.24, bf16[128,7168]{1,0:T(8,128)(2,1)} %bitcast.18, bf16[512,896]{1,0:T(8,128)(2,1)} %bitcast.20, bf16[2,64,512]{2,1,0:T(8,128)(2,1)} %bitcast.21), custom_call_target="tpu_custom_call" | custom-call | tf_op jit(solution)/shard_map/relay/pallas_call | solution.py:469
  76.0 0.0 copy-start
  76.0 1.6 %copy.11 = bf16[1,2,512,64]{2,3,1,0:T(8,128)(2,1)} copy(bf16[1,2,512,64]{2,3,1,0:T(8,128)(2,1)} %bitcast.22) | data formatting | bytes 262144
  77.6 2.2 %copy.12 = bf16[1,1,512,896]{3,2,1,0:T(8,128)(2,1)} copy(bf16[1,1,512,896]{3,2,1,0:T(8,128)(2,1)} %bitcast.19) | data formatting | bytes 1835008
  79.8 0.0 copy-done
  79.8 0.6 copy.13
Async XLA Ops:
  76.0 3.8 %copy-start = (f32[2,8,64]{2,1,0:T(8,128)S(1)}, f32[2,8,64]{2,1,0:T(8,128)}, u32[]{:S(2)}) copy-start(f32[2,8,64]{2,1,0:T(8,128)} %get-tuple-element.8) | copy-start | bytes 12292

commit v3 on v2

--- a/solution.py
+++ b/solution.py
@@ -11,6 +11,8 @@
 ZSIDE = 8
 ROW = 2 * ZSIDE
 LINE = ZSIDE // 2
+DEPTH = 2
+DIRECT = 2
 MESH = pl.DeviceIdType.MESH
 F32 = jnp.float32
 BF16 = jnp.bfloat16
@@ -48,6 +50,7 @@
     part_in,
     peer_out,
     peer_in,
+    fold_out,
     gate_src,
     gate_row,
     gate_mid,
@@ -238,30 +241,42 @@
             y_to * ROW + zc,
             before,
         )
-        hop.start()
         hops.append(hop)
+    hops[0].start()
+
+    way = 1 - 2 * core
+    deltas = [sign * step for step in range(1, LINE) for sign in (1, -1)] + [LINE, 0]
 
     def spread(turn):
-        hops[turn].wait_recv()
+        hops[turn].wait()
+        if turn + 1 < rounds:
+            hops[turn + 1].start()
         slot = source_of(y, turn) * ROW + zc
         own = fetched(
             row_in.at[turn, z_line * 2 + core], disp.at[slot], row_recv.at[turn]
         )
         own.start()
-
-        @pl.loop(1, ROW)
-        def _(offset):
-            peer = lax.rem(zc + offset, ROW)
-            block = ((peer // 2) % LINE) * 2 + peer % 2
-            remote(
-                row_in.at[turn, block],
-                disp.at[slot],
-                row_send.at[turn],
-                row_recv.at[turn],
-                y * ROW + peer,
-            ).start()
+        for delta in deltas:
+            z_to = lax.rem(z + ZSIDE + delta * way, ZSIDE)
+            for side in range(2):
+                if delta == 0 and side == 0:
+                    continue
+                c_to = lax.rem(core + side, 2)
+                remote(
+                    row_in.at[turn, lax.rem(z_to, LINE) * 2 + c_to],
+                    disp.at[slot],
+                    row_send.at[turn],
+                    row_recv.at[turn],
+                    y * ROW + z_to * 2 + c_to,
+                ).start()
 
     partner = jnp.where(y % 2 == 0, y + 1, y - 1)
+    parity = z_line % 2
+    upper = z_line // 2
+
+    def folds(step):
+        return LINE == 4 and step < yside - DIRECT
+
     twin = y * ROW + z * 2 + (1 - core)
     shares = []
 
@@ -313,6 +328,17 @@
     def pass_on(step):
         shares[step][1].wait_recv()
         peer_out[step] = (part[step, :, core] + part_in[step]).astype(BF16)
+        if folds(step):
+            near = z_base + z_line + 1 - 2 * parity
+            for pair in range(2):
+                remote(
+                    peer_out.at[step, 1 - parity + 2 * pair],
+                    peer_in.at[step, 1 + pair],
+                    peer_send.at[step, 1 + pair],
+                    peer_recv.at[step, 1 + pair],
+                    y * ROW + near * 2 + core,
+                ).start()
+            return
         for offset in range(1, LINE):
             target = lax.rem(z_line + offset, LINE)
             remote(
@@ -323,13 +349,36 @@
                 y * ROW + (z_base + target) * 2 + core,
             ).start()
 
+    def fold(step):
+        for pair in range(2):
+            arrived(peer_in.at[step, 1 + pair], peer_recv.at[step, 1 + pair])
+        away = parity + 2 * (1 - upper)
+        fold_out[step] = (
+            part[step, away, core]
+            + part_in[step, away]
+            + peer_in[step, 2 - upper].astype(F32)
+        ).astype(BF16)
+        remote(
+            fold_out.at[step],
+            peer_in.at[step, 3],
+            peer_send.at[step, 3],
+            peer_recv.at[step, 3],
+            y * ROW + (z_base + away) * 2 + core,
+        ).start()
+
     def finish(step):
         source = shares[step][0]
-        for offset in range(1, LINE):
-            arrived(peer_in.at[step, offset], peer_recv.at[step, offset])
+        if folds(step):
+            arrived(peer_in.at[step, 3], peer_recv.at[step, 3])
+        else:
+            for offset in range(1, LINE):
+                arrived(peer_in.at[step, offset], peer_recv.at[step, offset])
         whole = part[step, z_line, core] + part_in[step, z_line]
-        for offset in range(1, LINE):
-            whole = whole + peer_in[step, offset].astype(F32)
+        if folds(step):
+            whole = whole + peer_in[step, 1 + upper].astype(F32) + peer_in[step, 3].astype(F32)
+        else:
+            for offset in range(1, LINE):
+                whole = whole + peer_in[step, offset].astype(F32)
         gated = (gate_all[source, pl.ds(expert, 1), :] * whole).astype(BF16)
         turned_all[source] = lax.dot_general(
             gated, order, (((1,), (1,)), ((), ())), preferred_element_type=F32
@@ -362,32 +411,37 @@
             plan.append((False, turn - 1))
     plan.append((False, rounds - 1))
 
-    for turn in range(rounds):
+    spread(0)
+    arrived(gate_row, small_recv.at[0])
+    summed = gate_row[0]
+    for number in range(1, ROW):
+        summed = summed + gate_row[number]
+    gate_mid[...] = summed
+    column_cast(gate_mid, gate_all, 1)
+    for turn in range(1, min(DEPTH, rounds)):
         spread(turn)
-        if turn == 0:
-            arrived(gate_row, small_recv.at[0])
-            summed = gate_row[0]
-            for number in range(1, ROW):
-                summed = summed + gate_row[number]
-            gate_mid[...] = summed
-            column_cast(gate_mid, gate_all, 1)
-            for offset in range(1, LINE):
-                origin = lax.rem(z_line + LINE - offset, LINE)
-                arrived(saved_all.at[core, origin], saved_recv.at[offset])
-            share_saved = remote(
-                saved_all.at[core], saved_all.at[core], twin_sem.at[0], twin_sem.at[1], twin
-            )
-            share_saved.start()
+    for offset in range(1, LINE):
+        origin = lax.rem(z_line + LINE - offset, LINE)
+        arrived(saved_all.at[core, origin], saved_recv.at[offset])
+    share_saved = remote(
+        saved_all.at[core], saved_all.at[core], twin_sem.at[0], twin_sem.at[1], twin
+    )
+    share_saved.start()
     load_weight.wait()
     for step, (owned, turn) in enumerate(plan):
+        if owned and turn + DEPTH < rounds:
+            arrived(disp.at[pl.ds(0, ROW - 1)], row_send.at[turn])
+            spread(turn + DEPTH)
         receive(step, owned, turn)
         if step == 0:
             arrived(gate_all, small_recv.at[1])
         if step >= 1:
             pass_on(step - 1)
         grow(step)
-        if step >= 2:
-            finish(step - 2)
+        if step >= 2 and folds(step - 2):
+            fold(step - 2)
+        if step >= 3:
+            finish(step - 3)
     last = len(plan) - 1
     pass_on(last)
     arrived(score_col, small_recv.at[2])
@@ -395,8 +449,11 @@
     lines += [jnp.zeros((8 - experts, lanes), F32)]
     score_mid[...] = jnp.concatenate(lines, axis=0)
     row_cast(score_mid, score_row, 3)
-    if last >= 1:
-        finish(last - 1)
+    for step in range(max(last - 1, 0), last + 1):
+        if folds(step):
+            fold(step)
+    for step in range(max(last - 2, 0), last):
+        finish(step)
     finish(last)
     for micro in range(MICRO):
         hidden_out[micro] = jnp.concatenate(
@@ -428,8 +485,8 @@
 
     send_pick.wait_send()
     for turn in range(rounds):
-        hops[turn].wait_send()
-        arrived(disp.at[pl.ds(0, ROW - 1)], row_send.at[turn])
+        if turn + DEPTH >= rounds:
+            arrived(disp.at[pl.ds(0, ROW - 1)], row_send.at[turn])
         arrived(disp.at[pl.ds(0, ROW)], side_send.at[turn])
     for offset in range(1, LINE):
         arrived(saved_all.at[0, 0], saved_send.at[offset])
@@ -445,6 +502,12 @@
         (3, ROW - 1, score_row),
     ):
         arrived(block.at[pl.ds(0, count)], small_send.at[kind])
+
+
+def publish(hidden_ref, down_ref, gate_ref, hidden_to, down_to, gate_to):
+    hidden_to[...] = hidden_ref[...]
+    down_to[...] = down_ref[...]
+    gate_to[...] = gate_ref[...]
 
 
 def body(out_grad, expert_ids, gate_values, down_tiles, hidden_saved):
@@ -490,6 +553,7 @@
             pltpu.VMEM((steps, LINE, hid, lanes), F32),
             pltpu.VMEM((steps, LINE, hid, lanes), BF16),
             pltpu.VMEM((steps, LINE, hid, lanes), BF16),
+            pltpu.VMEM((steps, hid, lanes), BF16),
             pltpu.VMEM((8, lanes), F32),
             pltpu.VMEM((ROW, 8, lanes), F32),
             pltpu.VMEM((8, lanes), F32),
@@ -501,12 +565,7 @@
             pltpu.VMEM((yside, hid, lanes), BF16),
             dma((3,)),
             dma((2,)),
-            dma((rounds,)),
-            dma((rounds,)),
-            dma((rounds,)),
-            dma((rounds,)),
-            dma((rounds,)),
-            dma((rounds,)),
+            *[dma((rounds,)) for _ in range(6)],
             dma((LINE,)),
             dma((LINE,)),
             dma((2,)),
@@ -528,6 +587,17 @@
         down_tiles.reshape(tile_rows, tile_cols),
         saved,
     )
+    hidden_grad, down_grad, gate_grad = pl.pallas_call(
+        publish,
+        out_shape=tuple(
+            jax.ShapeDtypeStruct(value.shape, value.dtype)
+            for value in (hidden_grad, down_grad, gate_grad)
+        ),
+        in_specs=[vmem, vmem, vmem],
+        out_specs=(vmem, vmem, vmem),
+        compiler_params=pltpu.CompilerParams(vmem_limit_bytes=62 * 2**20),
+        name="publish",
+    )(hidden_grad, down_grad, gate_grad)
     return (
         hidden_grad.reshape(1, micro, hid, slots).transpose(0, 1, 3, 2),
         down_grad.reshape(1, 1, tile_rows, tile_cols),

time: 80.6 us -> 76.9 us (0.954); the launches traced: 80.4 us -> 75.8 us
  local copies, waits for them, and re-layouts: 4.35 us -> 0 us
    unnamed x5 -> x0, local copies, waits for them, and re-layouts: 4.35 us -> none
    pallas_call x1, Pallas kernels: 75.4 us -> 73 us  [body(): pl.pallas_call(lambda *refs: relay_kernel((pipes, yside), *refs), out_sha...]
    pallas_call x0 -> x1, Pallas kernels: none -> 2.21 us  [body(): pl.pallas_call(publish, out_shape=tuple((jax.ShapeDtypeStruct(value.shape...]
where the time goes in v3:
time: 76.9 us; the launch traced here: 75.8 us
  Pallas kernels  75.2 us (98%)
    pallas_call x1, Pallas kernels, body(): pl.pallas_call(lambda *refs: relay_kernel((pipes, yside), *refs), out_sha...  73 us
    pallas_call x1, Pallas kernels, body(): pl.pallas_call(publish, out_shape=tuple((jax.ShapeDtypeStruct(value.shape...  2.21 us

profile of v3, /device:TPU:7, one launch (start us, length us, event | category | flops | bytes accessed | tf_op | source)
XLA Modules:
  0.0 75.8 jit_solution(18153894366434624369)
XLA Ops:
  0.6 73.0 %relay.1 = (bf16[2,64,512]{2,1,0:T(8,128)(2,1)}, bf16[512,896]{1,0:T(8,128)(2,1)}, f32[2,8,64]{2,1,0:T(8,128)}) custom-call(s32[2,8,64]{2,1,0:T(8,128)} %bitcast.21, f32[2,8,64]{2,1,0:T(8,128)} %bitcast.22, bf16[128,7168]{1,0:T(8,128)(2,1)} %bitcast.18, bf16[512,896]{1,0:T(8,128)(2,1)} %bitcast.19, bf16[2,64,512]{2,1,0:T(8,128)(2,1)} %bitcast.20), custom_call_target="tpu_custom_call" | custom-call | tf_op jit(solution)/shard_map/relay/pallas_call | solution.py:532
  73.6 2.2 %publish.1 = (bf16[2,64,512]{2,1,0:T(8,128)(2,1)}, bf16[512,896]{1,0:T(8,128)(2,1)}, f32[2,8,64]{2,1,0:T(8,128)}) custom-call(bf16[2,64,512]{2,1,0:T(8,128)(2,1)} %get-tuple-element.9.hidden_ref, bf16[512,896]{1,0:T(8,128)(2,1)} %get-tuple-element.10.down_ref, f32[2,8,64]{2,1,0:T(8,128)} %get-tuple-element.11.gate_ref), custom_call_target="tpu_custom_call" | custom-call | tf_op jit(solution)/shard_map/publish/pallas_call | solution.py:590

commit v4 on v3

--- a/solution.py
+++ b/solution.py
@@ -46,6 +46,7 @@
     disp,
     saved_all,
     total,
+    down_held,
     part,
     part_in,
     peer_out,
@@ -402,7 +403,8 @@
         if step < yside - 1:
             total[...] = update
         else:
-            down_out[...] = update.astype(BF16)
+            down_held[...] = update.astype(BF16)
+            fetched(down_held, down_out, load_sem.at[3]).start()
 
     plan = []
     for turn in range(rounds):
@@ -483,6 +485,7 @@
     for micro in range(MICRO):
         gate_out[micro] = result[:, micro * tok_dev : (micro + 1) * tok_dev]
 
+    arrived(down_held, load_sem.at[3])
     send_pick.wait_send()
     for turn in range(rounds):
         if turn + DEPTH >= rounds:
@@ -504,10 +507,23 @@
         arrived(block.at[pl.ds(0, count)], small_send.at[kind])
 
 
-def publish(hidden_ref, down_ref, gate_ref, hidden_to, down_to, gate_to):
-    hidden_to[...] = hidden_ref[...]
-    down_to[...] = down_ref[...]
-    gate_to[...] = gate_ref[...]
+def publish(hidden_ref, down_ref, gate_ref, hidden_to, down_to, gate_to, hidden, down, gate, sem_in, sem_out):
+    half = down.shape[0] // 2
+    moves = [
+        (down_ref.at[pl.ds(0, half)], down.at[pl.ds(0, half)], down_to.at[pl.ds(0, half)]),
+        (down_ref.at[pl.ds(half, half)], down.at[pl.ds(half, half)], down_to.at[pl.ds(half, half)]),
+        (hidden_ref, hidden, hidden_to),
+        (gate_ref, gate, gate_to),
+    ]
+    loads = [fetched(a, b, sem_in.at[k]) for k, (a, b, _) in enumerate(moves)]
+    stores = [fetched(b, c, sem_out.at[k]) for k, (_, b, c) in enumerate(moves)]
+    for copy in loads:
+        copy.start()
+    for load, store in zip(loads, stores):
+        load.wait()
+        store.start()
+    for store in stores:
+        store.wait()
 
 
 def body(out_grad, expert_ids, gate_values, down_tiles, hidden_saved):
@@ -537,7 +553,7 @@
             jax.ShapeDtypeStruct((micro, topk, tok_dev), F32),
         ),
         in_specs=[vmem, vmem, far, far, far],
-        out_specs=(vmem, vmem, vmem),
+        out_specs=(vmem, far, vmem),
         scratch_shapes=[
             pltpu.VMEM((tokens, width), BF16),
             pltpu.VMEM((tile_rows, tile_cols), BF16),
@@ -549,6 +565,7 @@
             pltpu.VMEM((devices, UNIT, tile_cols), BF16),
             pltpu.VMEM((2, LINE, yside, hid, lanes), BF16),
             pltpu.VMEM((tile_rows, tile_cols), F32),
+            pltpu.VMEM((tile_rows, tile_cols), BF16),
             pltpu.VMEM((steps, LINE, 2, hid, lanes), F32),
             pltpu.VMEM((steps, LINE, hid, lanes), F32),
             pltpu.VMEM((steps, LINE, hid, lanes), BF16),
@@ -563,7 +580,7 @@
             pltpu.VMEM((8, lanes), F32),
             pltpu.VMEM((ROW, 8, lanes), F32),
             pltpu.VMEM((yside, hid, lanes), BF16),
-            dma((3,)),
+            dma((4,)),
             dma((2,)),
             *[dma((rounds,)) for _ in range(6)],
             dma((LINE,)),
@@ -593,8 +610,15 @@
             jax.ShapeDtypeStruct(value.shape, value.dtype)
             for value in (hidden_grad, down_grad, gate_grad)
         ),
-        in_specs=[vmem, vmem, vmem],
-        out_specs=(vmem, vmem, vmem),
+        in_specs=[far, far, far],
+        out_specs=(far, far, far),
+        scratch_shapes=[
+            pltpu.VMEM((micro, hid, slots), BF16),
+            pltpu.VMEM((tile_rows, tile_cols), BF16),
+            pltpu.VMEM((micro, topk, tok_dev), F32),
+            dma((4,)),
+            dma((4,)),
+        ],
         compiler_params=pltpu.CompilerParams(vmem_limit_bytes=62 * 2**20),
         name="publish",
     )(hidden_grad, down_grad, gate_grad)

time: 76.9 us -> 76.4 us (level)
  no operation moved by 1% of the time
where the time goes in v4:
time: 76.4 us; the launch traced here: 75.3 us
  Pallas kernels  74.7 us (98%)
    pallas_call x1, Pallas kernels, body(): pl.pallas_call(lambda *refs: relay_kernel((pipes, yside), *refs), out_sha...  72.7 us
    pallas_call x1, Pallas kernels, body(): pl.pallas_call(publish, out_shape=tuple((jax.ShapeDtypeStruct(value.shape...  2.05 us

profile of v4, /device:TPU:7, one launch (start us, length us, event | category | flops | bytes accessed | tf_op | source)
XLA Modules:
  0.0 75.3 jit_solution(8211654655740699901)
XLA Ops:
  0.6 72.7 %relay.1 = (bf16[2,64,512]{2,1,0:T(8,128)(2,1)}, bf16[512,896]{1,0:T(8,128)(2,1)}, f32[2,8,64]{2,1,0:T(8,128)}) custom-call(s32[2,8,64]{2,1,0:T(8,128)} %bitcast.21, f32[2,8,64]{2,1,0:T(8,128)} %bitcast.22, bf16[128,7168]{1,0:T(8,128)(2,1)} %bitcast.18, bf16[512,896]{1,0:T(8,128)(2,1)} %bitcast.19, bf16[2,64,512]{2,1,0:T(8,128)(2,1)} %bitcast.20), custom_call_target="tpu_custom_call" | custom-call | tf_op jit(solution)/shard_map/relay/pallas_call | solution.py:548
  73.3 2.0 %publish.1 = (bf16[2,64,512]{2,1,0:T(8,128)(2,1)}, bf16[512,896]{1,0:T(8,128)(2,1)}, f32[2,8,64]{2,1,0:T(8,128)}) custom-call(bf16[2,64,512]{2,1,0:T(8,128)(2,1)} %get-tuple-element.9.hidden_ref, bf16[512,896]{1,0:T(8,128)(2,1)} %get-tuple-element.10.down_ref, f32[2,8,64]{2,1,0:T(8,128)} %get-tuple-element.11.gate_ref), custom_call_target="tpu_custom_call" | custom-call | tf_op jit(solution)/shard_map/publish/pallas_call | solution.py:607
